TPU v7x, 128 devices: a whole 4x4x4 slice. The times are simulated.
128 devices in a mesh: ctx: 64 (over x_lo, y, z, core), head: 2 (over x_hi).
Axes of the slice: x: 4 (x_hi: 2, x_lo: 2; x = x_hi * 2 + x_lo), y: 4, z: 4, core: 2. Of those that a mesh axis runs over, the one named last changes fastest.
Arguments:
- queries: bfloat16 [32768, 1024], P(('ctx', 'head')), may hold values from -9 to 9
- keys_in: bfloat16 [32768, 1024], P(('ctx', 'head')), may hold values from -9 to 9
- values: bfloat16 [32768, 1024], P(('ctx', 'head')), may hold values from -6 to 6
- d_out: bfloat16 [32768, 1024], P(('ctx', 'head')), may hold values from -6 to 6
- pair_blocks: int32 [512, 16], replicated, may hold values from 0 to 511, as said below
- pair_count: int32 [512], replicated, may hold values from 1 to 16, as said below
Outputs:
- d_queries: bfloat16 [32768, 1024], P(('ctx', 'head'))
- d_keys: bfloat16 [32768, 1024], P(('ctx', 'head'))
- d_values: bfloat16 [32768, 1024], P(('ctx', 'head'))
Inputs may be any that keep to these rules, and one draw needn't show every extreme that they name: `pair_blocks`: entry 0 of row b is b itself; every entry of row b is a block of a person within 2 persons of the person of block b (a person's tokens are 512 in a row). Entries may repeat. Only the first pair_count[b] entries of row b are listed.
All inputs are finite; a program needn't handle non-finite values.
Results may differ from a plain program's by a relative error of at most 0.012.
The roundings to bfloat16 on the way count: a program that leaves them out, or rounds other values in their place, can miss the bound.
Values may be sent and summed in bfloat16 or wider, within the bound.
A program may use at most 192 MiB of HBM per device.

v0:
```python
import jax
import jax.numpy as jnp
from jax import lax
from jax.sharding import PartitionSpec as P

HEAD_DIM = 64
BLOCK = 64
REACH = 2
masked_value = -1e30


def shifted(shard, axis, by):
    peers = lax.axis_size(axis)
    pairs = [(i, i + by) for i in range(peers) if 0 <= i + by < peers]
    return lax.ppermute(shard, axis, pairs)


def expand_mask(block_mask, block_rows):
    count_rows, count_cols = block_mask.shape
    widened = jnp.broadcast_to(
        block_mask[:, None, :, None], (count_rows, block_rows, count_cols, block_rows)
    )
    return widened.reshape(count_rows * block_rows, count_cols * block_rows)


def block_listing(pair_blocks, pair_count, first_query, query_blocks, first_key, key_blocks):
    lists = lax.dynamic_slice_in_dim(pair_blocks, first_query, query_blocks, 0)
    counts = lax.dynamic_slice_in_dim(pair_count, first_query, query_blocks, 0)
    live_slots = jnp.arange(lists.shape[1], dtype=jnp.int32)[None, :] < counts[:, None]
    wanted = first_key + jnp.arange(key_blocks, dtype=jnp.int32)
    return jnp.any((lists[:, :, None] == wanted[None, None, :]) & live_slots[:, :, None], axis=1)


def masked_scores(query_heads, key_heads, token_mask, score_scale):
    product = jnp.einsum("qhd,khd->hqk", query_heads, key_heads, preferred_element_type=jnp.float32)
    return jnp.where(token_mask[None], product * score_scale, masked_value)


def score_grads(probs, dout_heads, value_heads, row_delta):
    d_probs = jnp.einsum(
        "qhd,khd->hqk", dout_heads, value_heads, preferred_element_type=jnp.float32
    )
    return (probs * (d_probs - row_delta[:, :, None])).astype(jnp.bfloat16)


def key_value_grads(d_scores, probs, query_heads, dout_heads):
    key_part = jnp.einsum("hqk,qhd->khd", d_scores, query_heads, preferred_element_type=jnp.float32)
    value_part = jnp.einsum(
        "hqk,qhd->khd", probs.astype(jnp.bfloat16), dout_heads, preferred_element_type=jnp.float32
    )
    return jnp.stack([key_part, value_part]).astype(jnp.bfloat16)


def widen_part(rounded):
    return lax.optimization_barrier(rounded).astype(jnp.float32)


def on_device(queries, keys_in, values, d_out, pair_blocks, pair_count):
    entering = jnp.stack([queries, keys_in, values, d_out])
    head_local = lax.all_to_all(entering, "head", split_axis=2, concat_axis=1, tiled=True)
    frames = head_local.shape[1]
    feature_cols = head_local.shape[2]
    heads_dev = feature_cols // HEAD_DIM
    blocks_dev = frames // BLOCK
    window_span = 2 * REACH + 1
    score_scale = HEAD_DIM ** (-0.5)
    position = lax.axis_index("ctx")

    def split_heads(matrix):
        return matrix.reshape(frames, heads_dev, HEAD_DIM)

    query_heads = split_heads(head_local[0])
    dout_heads = split_heads(head_local[3])
    window_mask = block_listing(
        pair_blocks,
        pair_count,
        position * blocks_dev,
        blocks_dev,
        (position - REACH) * blocks_dev,
        window_span * blocks_dev,
    )
    key_pair = head_local[1:3]
    remote_tiles = {0: key_pair}
    for direction in (1, -1):
        current = key_pair
        for stride in range(1, REACH + 1):
            current = shifted(current, "ctx", direction)
            remote_tiles[-direction * stride] = current
    offsets = [0]
    for stride in range(1, REACH + 1):
        offsets = offsets + [-stride, stride]
    tile_masks = {}
    for offset in offsets:
        column = (offset + REACH) * blocks_dev
        tile_masks[offset] = expand_mask(window_mask[:, column : column + blocks_dev], BLOCK)
    row_top = jnp.full((heads_dev, frames), masked_value, jnp.float32)
    row_total = jnp.zeros((heads_dev, frames), jnp.float32)
    tile_scores = {}
    for offset in offsets:
        scores = masked_scores(
            query_heads, split_heads(remote_tiles[offset][0]), tile_masks[offset], score_scale
        )
        tile_scores[offset] = scores
        new_top = jnp.maximum(row_top, jnp.max(scores, axis=-1))
        kept = jnp.where(tile_masks[offset][None], jnp.exp(scores - new_top[:, :, None]), 0.0)
        row_total = row_total * jnp.exp(row_top - new_top) + jnp.sum(kept, axis=-1)
        row_top = new_top
    log_total = row_top + jnp.log(row_total)
    attention = jnp.zeros((frames, heads_dev, HEAD_DIM), jnp.float32)
    tile_probs = {}
    for offset in offsets:
        probs = jnp.where(
            tile_masks[offset][None], jnp.exp(tile_scores[offset] - log_total[:, :, None]), 0.0
        )
        tile_probs[offset] = probs
        attention = attention + jnp.einsum(
            "hqk,khd->qhd",
            probs.astype(jnp.bfloat16),
            split_heads(remote_tiles[offset][1]),
            preferred_element_type=jnp.float32,
        )
    row_delta = jnp.sum(dout_heads.astype(jnp.float32) * attention, axis=-1).T
    query_grad = jnp.zeros((frames, heads_dev, HEAD_DIM), jnp.float32)
    tile_parts = {}
    for offset in offsets:
        key_heads = split_heads(remote_tiles[offset][0])
        d_scores = score_grads(
            tile_probs[offset], dout_heads, split_heads(remote_tiles[offset][1]), row_delta
        )
        query_grad = query_grad + jnp.einsum(
            "hqk,khd->qhd", d_scores, key_heads, preferred_element_type=jnp.float32
        )
        tile_parts[offset] = key_value_grads(d_scores, tile_probs[offset], query_heads, dout_heads)
    collected = widen_part(tile_parts[0])
    for offset in offsets[1:]:
        arrived = shifted(tile_parts[offset], "ctx", offset)
        collected = collected + arrived.astype(jnp.float32)
    query_out = (query_grad * score_scale).astype(jnp.bfloat16).reshape(frames, feature_cols)
    key_out = (collected[0] * score_scale).astype(jnp.bfloat16).reshape(frames, feature_cols)
    value_out = collected[1].astype(jnp.bfloat16).reshape(frames, feature_cols)
    leaving = lax.all_to_all(
        jnp.stack([query_out, key_out, value_out]), "head", split_axis=1, concat_axis=2, tiled=True
    )
    return (leaving[0], leaving[1], leaving[2])


def solution(mesh):
    placed = (
        P(("ctx", "head"), None),
        P(("ctx", "head"), None),
        P(("ctx", "head"), None),
        P(("ctx", "head"), None),
        P(),
        P(),
    )
    return jax.shard_map(
        on_device,
        mesh=mesh,
        in_specs=placed,
        out_specs=(P(("ctx", "head"), None), P(("ctx", "head"), None), P(("ctx", "head"), None)),
        check_vma=False,
    )
```

profile of v0, /device:TPU:121, one launch (start us, length us, event | category | flops | bytes accessed | tf_op | source)
XLA Modules:
  0.0 277.8 jit_solution(14616400120939298782)
XLA Ops:
  5.0 4.0 %all-to-all-start = ((bf16[4,256,1024]{1,0,2:T(4,128)(2,1)}), bf16[4,256,1024]{1,0,2:T(4,128)(2,1)S(1)}, u32[]{:S(2)}, u32[]{:S(2)}) async-start(bf16[4,256,1024]{1,0,2:T(4,128)(2,1)} %copy.108), calls=%async_computation | async-start | bytes 4194304 | tf_op jit(solution)/shard_map/all_to_all | solution.py:60
  10.0 24.4 %all-to-all-done = bf16[4,256,1024]{1,0,2:T(4,128)(2,1)S(1)} async-done(((bf16[4,256,1024]{1,0,2:T(4,128)(2,1)}), bf16[4,256,1024]{1,0,2:T(4,128)(2,1)S(1)}, u32[]{:S(2)}, u32[]{:S(2)}) %all-to-all-start) | async-done | bytes 2097184 | tf_op jit(solution)/shard_map/all_to_all | solution.py:60
  35.8 3.7 %copy.176 = bf16[4,256,2,512]{1,2,3,0:T(2,128)(2,1)S(1)} copy(bf16[4,256,2,512]{1,0,3,2:T(4,128)(2,1)} %bitcast.163) | data formatting | bytes 4194304 | tf_op jit(solution)/shard_map/all_to_all | solution.py:60
  41.8 3.8 %collective-permute-start.1 = (bf16[2,512,512]{1,2,0:T(8,128)(2,1)}, bf16[2,512,512]{1,2,0:T(8,128)(2,1)}, u32[]{:S(2)}, u32[]{:S(2)}) collective-permute-start(bf16[2,512,512]{1,2,0:T(8,128)(2,1)} %slice.97), channel_id=1, source_target_pairs={{2,0},{4,2},{6,4},{8,6},{10,8},{12,10},{14,12},{16,14},{18,16},{20... | collective-permute-start | bytes 3145736 | tf_op jit(solution)/shard_map/ppermute | solution.py:15
  45.7 6.2 %collective-permute-start = (bf16[2,512,512]{1,2,0:T(8,128)(2,1)}, bf16[2,512,512]{1,2,0:T(8,128)(2,1)}, u32[]{:S(2)}, u32[]{:S(2)}) collective-permute-start(bf16[2,512,512]{1,2,0:T(8,128)(2,1)} %slice.97), channel_id=1, source_target_pairs={{0,2},{2,4},{4,6},{6,8},{8,10},{10,12},{12,14},{14,16},{16,18},{18... | collective-permute-start | bytes 3145736 | tf_op jit(solution)/shard_map/ppermute | solution.py:15
  74.1 8.1 %collective-permute-start.2 = (bf16[2,512,512]{1,2,0:T(8,128)(2,1)}, bf16[2,512,512]{1,2,0:T(8,128)(2,1)S(1)}, u32[]{:S(2)}, u32[]{:S(2)}) collective-permute-start(bf16[2,512,512]{1,2,0:T(8,128)(2,1)} %collective-permute-done), channel_id=1, source_target_pairs={{0,2},{2,4},{4,6},{6,8},{8,10},{10,12},{12,14},{14,16},{16,18},{18... | collective-permute-start | bytes 3145736 | tf_op jit(solution)/shard_map/ppermute | solution.py:15
  86.5 4.9 %collective-permute-done.3 = bf16[2,512,512]{1,2,0:T(8,128)(2,1)S(1)} collective-permute-done((bf16[2,512,512]{1,2,0:T(8,128)(2,1)}, bf16[2,512,512]{1,2,0:T(8,128)(2,1)S(1)}, u32[]{:S(2)}, u32[]{:S(2)}) %collective-permute-start.3) | collective-permute-done | bytes 1048608 | tf_op jit(solution)/shard_map/ppermute | solution.py:15
  91.5 4.7 %fusion.9 = (f32[8,512]{1,0:T(8,128)S(1)}, f32[8,512,512]{1,2,0:T(8,128)}) fusion(pred[512,512]{0,1:T(8,128)(4,1)S(1)} %broadcast_in_dim.159, bf16[512,8,64]{0,2,1:T(8,128)(2,1)S(1)} %reshape_squeeze.47, bf16[512,8,64]{0,2,1:T(8,128)(2,1)S(1)} %bitcast.170), kind=kOutput, calls=%fused_computation.29 | convolution fusion | flops 274722816 | bytes 9715712 | tf_op jit(solution)/shard_map/qhd,khd->hqk/dot_general | solution.py:35
  96.3 4.7 %fusion.8 = (f32[8,512]{1,0:T(8,128)S(1)}, f32[8,512,512]{1,2,0:T(8,128)}) fusion(pred[512,512]{0,1:T(8,128)(4,1)S(1)} %broadcast_in_dim.156, bf16[512,8,64]{0,2,1:T(8,128)(2,1)S(1)} %reshape_squeeze.47, bf16[512,8,64]{0,2,1:T(8,128)(2,1)S(1)} %bitcast.164), kind=kOutput, calls=%fused_computation.28 | convolution fusion | flops 274722816 | bytes 9715712 | tf_op jit(solution)/shard_map/qhd,khd->hqk/dot_general | solution.py:35
  103.6 7.9 %select_reduce_fusion = (f32[8,512]{1,0:T(8,128)S(1)}, f32[8,512]{1,0:T(8,128)S(1)}) fusion(f32[8,512,512]{1,2,0:T(8,128)} %get-tuple-element.29, f32[8,512]{1,0:T(8,128)S(1)} %get-tuple-element.3, pred[512,512]{0,1:T(8,128)(4,1)S(1)} %broadcast_in_dim.159, f32[8,512]{1,0:T(8,128)S(1)} %get-tuple-element.4, f32[8,512,512]{1,2,0:T(8,128)} %get-tuple-element.31, ...), kind=kLoop, calls=%fused_computation.10 | loop fusion | flops 20963328 | bytes 17367040 | tf_op jit(solution)/shard_map/reduce_sum | solution.py:106
  111.5 4.0 %select_reduce_fusion.2 = (f32[8,512]{1,0:T(8,128)S(1)}, f32[8,512]{1,0:T(8,128)S(1)}) fusion(f32[8,512,512]{1,2,0:T(8,128)S(1)} %get-tuple-element.33, f32[8,512]{1,0:T(8,128)S(1)} %get-tuple-element.5, pred[512,512]{0,1:T(8,128)(4,1)S(1)} %broadcast_in_dim.153, f32[8,512]{1,0:T(8,128)S(1)} %get-tuple-element.6, f32[8,512,512]{1,2,0:T(8,128)S(1)} %get-tuple-element.35, ...), kind=kLoop, calls=%fused_computation.12 | loop fusion | flops 20963328 | bytes 17367040 | tf_op jit(solution)/shard_map/reduce_sum | solution.py:106
  115.5 6.5 %fusion.26 = bf16[1,512,8,64]{1,3,2,0:T(8,128)(2,1)} fusion(bf16[512,8,64]{0,2,1:T(8,128)(2,1)S(1)} %reshape_squeeze.52, f32[8,512,512]{1,2,0:T(8,128)} %get-tuple-element.29, f32[8,512]{1,0:T(8,128)S(1)} %log_add_fusion, pred[512,512]{0,1:T(8,128)(4,1)S(1)} %broadcast_in_dim.159), kind=kOutput, calls=%fused_computation.66 | convolution fusion | flops 279183360 | bytes 9715712 | tf_op jit(solution)/shard_map/hqk,qhd->khd/dot_general | solution.py:48
  122.0 6.5 %fusion.24 = bf16[1,512,8,64]{1,3,2,0:T(8,128)(2,1)} fusion(bf16[512,8,64]{0,2,1:T(8,128)(2,1)S(1)} %reshape_squeeze.52, f32[8,512,512]{1,2,0:T(8,128)} %get-tuple-element.31, f32[8,512]{1,0:T(8,128)S(1)} %log_add_fusion, pred[512,512]{0,1:T(8,128)(4,1)S(1)} %broadcast_in_dim.156), kind=kOutput, calls=%fused_computation.64 | convolution fusion | flops 279183360 | bytes 9715712 | tf_op jit(solution)/shard_map/hqk,qhd->khd/dot_general | solution.py:48
  128.5 5.8 %fusion.36 = f32[8,64,512]{2,1,0:T(8,128)S(1)} fusion(bf16[512,8,64]{0,2,1:T(8,128)(2,1)S(1)} %bitcast.185, f32[8,512,512]{1,2,0:T(8,128)} %get-tuple-element.29, f32[8,512]{1,0:T(8,128)S(1)} %log_add_fusion, pred[512,512]{0,1:T(8,128)(4,1)S(1)} %broadcast_in_dim.159), kind=kOutput, calls=%fused_computation.82 | convolution fusion | flops 278921216 | bytes 10240000 | tf_op jit(solution)/shard_map/hqk,khd->qhd/dot_general | solution.py:116
  141.8 5.9 %fusion.16 = f32[512,8]{0,1:T(8,128)S(1)} fusion(f32[8,64,512]{2,1,0:T(8,128)S(1)} %fusion.36, f32[8,64,512]{2,1,0:T(8,128)S(1)} %convolution_add_fusion.4, bf16[512,8,64]{0,2,1:T(8,128)(2,1)S(1)} %bitcast.187, bf16[512,8,64]{0,2,1:T(8,128)(2,1)S(1)} %reshape_squeeze.52, f32[8,512,512]{1,2,0:T(8,128)} %get-tuple-element.31, f32[8,512]{1,0:T(8,128)S(1)} %log_add_fusion, ...), kind=kOutput, calls=%fused_computation.56 | convolution fusion | flops 280227840 | bytes 11829248 | tf_op jit(solution)/shard_map/hqk,khd->qhd/dot_general | solution.py:116
  147.7 6.8 %multiply_convert_fusion = bf16[8,512,512]{1,2,0:T(8,128)(2,1)} fusion(f32[8,512,512]{1,2,0:T(8,128)} %get-tuple-element.29, f32[8,512]{1,0:T(8,128)S(1)} %bitcast.193, f32[8,512]{1,0:T(8,128)S(1)} %log_add_fusion, pred[512,512]{0,1:T(8,128)(4,1)S(1)} %broadcast_in_dim.159, bf16[512,8,64]{0,2,1:T(8,128)(2,1)S(1)} %reshape_squeeze.52, ...), kind=kOutput, calls=%fused_computation | convolution fusion | flops 283115520 | bytes 13926400 | tf_op jit(solution)/shard_map/qhd,khd->hqk/dot_general | solution.py:40
  154.5 6.8 %multiply_convert_fusion.1 = bf16[8,512,512]{1,2,0:T(8,128)(2,1)} fusion(f32[8,512,512]{1,2,0:T(8,128)} %get-tuple-element.31, f32[8,512]{1,0:T(8,128)S(1)} %bitcast.194, f32[8,512]{1,0:T(8,128)S(1)} %log_add_fusion, pred[512,512]{0,1:T(8,128)(4,1)S(1)} %broadcast_in_dim.156, bf16[512,8,64]{0,2,1:T(8,128)(2,1)S(1)} %reshape_squeeze.52, ...), kind=kOutput, calls=%fused_computation.1 | convolution fusion | flops 283115520 | bytes 13926400 | tf_op jit(solution)/shard_map/qhd,khd->hqk/dot_general | solution.py:40
  164.6 4.8 %multiply_convert_fusion.2 = bf16[8,512,512]{1,2,0:T(8,128)(2,1)} fusion(f32[8,512,512]{1,2,0:T(8,128)S(1)} %get-tuple-element.33, f32[8,512]{1,0:T(8,128)S(1)} %bitcast.195, f32[8,512]{1,0:T(8,128)S(1)} %log_add_fusion, pred[512,512]{0,1:T(8,128)(4,1)S(1)} %broadcast_in_dim.153, bf16[512,8,64]{0,2,1:T(8,128)(2,1)S(1)} %reshape_squeeze.52, ...), kind=kOutput, calls=%fused_computation.2 | convolution fusion | flops 283115520 | bytes 13926400 | tf_op jit(solution)/shard_map/qhd,khd->hqk/dot_general | solution.py:40
  191.3 3.6 %collective-permute-start.6 = (bf16[2,512,8,64]{1,3,2,0:T(8,128)(2,1)}, bf16[2,512,8,64]{1,3,2,0:T(8,128)(2,1)}, u32[]{:S(2)}, u32[]{:S(2)}) collective-permute-start(bf16[2,512,8,64]{1,3,2,0:T(8,128)(2,1)} %pad_maximum_fusion.5), channel_id=1, source_target_pairs={{4,0},{6,2},{8,4},{10,6},{12,8},{14,10},{16,12},{18,14},{20,16},{2... | collective-permute-start | bytes 3145736 | tf_op jit(solution)/shard_map/ppermute | solution.py:15
  197.3 11.0 %collective-permute-start.5 = (bf16[2,512,8,64]{1,3,2,0:T(8,128)(2,1)}, bf16[2,512,8,64]{1,3,2,0:T(8,128)(2,1)}, u32[]{:S(2)}, u32[]{:S(2)}) collective-permute-start(bf16[2,512,8,64]{1,3,2,0:T(8,128)(2,1)} %pad_maximum_fusion.4), channel_id=1, source_target_pairs={{0,2},{2,4},{4,6},{6,8},{8,10},{10,12},{12,14},{14,16},{16,18},{18... | collective-permute-start | bytes 3145736 | tf_op jit(solution)/shard_map/ppermute | solution.py:15
  217.6 5.7 %collective-permute-done.5 = bf16[2,512,8,64]{1,3,2,0:T(8,128)(2,1)} collective-permute-done((bf16[2,512,8,64]{1,3,2,0:T(8,128)(2,1)}, bf16[2,512,8,64]{1,3,2,0:T(8,128)(2,1)}, u32[]{:S(2)}, u32[]{:S(2)}) %collective-permute-start.5) | collective-permute-done | bytes 1048608 | tf_op jit(solution)/shard_map/ppermute | solution.py:15
  223.3 10.5 %collective-permute-done.4 = bf16[2,512,8,64]{1,3,2,0:T(8,128)(2,1)} collective-permute-done((bf16[2,512,8,64]{1,3,2,0:T(8,128)(2,1)}, bf16[2,512,8,64]{1,3,2,0:T(8,128)(2,1)}, u32[]{:S(2)}, u32[]{:S(2)}) %collective-permute-start.4) | collective-permute-done | bytes 1048608 | tf_op jit(solution)/shard_map/ppermute | solution.py:15
  241.1 3.6 %pad_maximum_fusion.1 = bf16[3,512,512]{2,0,1:T(4,128)(2,1)S(1)} fusion(bf16[1,512,512]{2,0,1:T(2,128)(2,1)S(1)} %copy.143, bf16[1,512,512]{2,0,1:T(2,128)(2,1)S(1)} %copy.142, bf16[1,512,512]{2,0,1:T(2,128)(2,1)S(1)} %copy.141), kind=kLoop, calls=%fused_computation.31 | loop fusion | flops 4718592 | bytes 3145728 | tf_op jit(solution)/shard_map/stack | solution.py:142
  244.7 25.3 %all_to_all.30 = bf16[3,512,512]{2,0,1:T(4,128)(2,1)S(1)} all-to-all(bf16[3,512,512]{2,0,1:T(4,128)(2,1)S(1)} %pad_maximum_fusion.1), channel_id=1, replica_groups=mesh['ctx'=64,'head'=2] {'head'}, dimensions={1} | all-to-all | bytes 3145728 | tf_op jit(solution)/shard_map/all_to_all | solution.py:141
  (121 shorter events, 96.7 us)
Async XLA Ops:
  0.6 8.4 %copy-start = (s32[512,16]{0,1:T(8,128)S(1)}, s32[512,16]{0,1:T(8,128)}, u32[]{:S(2)}) copy-start(s32[512,16]{0,1:T(8,128)} %param.10) | copy-start | bytes 98308
  5.0 29.4 %all-to-all-start = ((bf16[4,256,1024]{1,0,2:T(4,128)(2,1)}), bf16[4,256,1024]{1,0,2:T(4,128)(2,1)S(1)}, u32[]{:S(2)}, u32[]{:S(2)}) async-start(bf16[4,256,1024]{1,0,2:T(4,128)(2,1)} %copy.108), calls=%async_computation | async-start | bytes 4194304 | tf_op jit(solution)/shard_map/all_to_all | solution.py:60
  41.8 29.1 %collective-permute-start.1 = (bf16[2,512,512]{1,2,0:T(8,128)(2,1)}, bf16[2,512,512]{1,2,0:T(8,128)(2,1)}, u32[]{:S(2)}, u32[]{:S(2)}) collective-permute-start(bf16[2,512,512]{1,2,0:T(8,128)(2,1)} %slice.97), channel_id=1, source_target_pairs={{2,0},{4,2},{6,4},{8,6},{10,8},{12,10},{14,12},{16,14},{18,16},{20... | collective-permute-start | bytes 3145736 | tf_op jit(solution)/shard_map/ppermute | solution.py:15
  45.7 28.4 %collective-permute-start = (bf16[2,512,512]{1,2,0:T(8,128)(2,1)}, bf16[2,512,512]{1,2,0:T(8,128)(2,1)}, u32[]{:S(2)}, u32[]{:S(2)}) collective-permute-start(bf16[2,512,512]{1,2,0:T(8,128)(2,1)} %slice.97), channel_id=1, source_target_pairs={{0,2},{2,4},{4,6},{6,8},{8,10},{10,12},{12,14},{14,16},{16,18},{18... | collective-permute-start | bytes 3145736 | tf_op jit(solution)/shard_map/ppermute | solution.py:15
  70.9 20.5 %collective-permute-start.3 = (bf16[2,512,512]{1,2,0:T(8,128)(2,1)}, bf16[2,512,512]{1,2,0:T(8,128)(2,1)S(1)}, u32[]{:S(2)}, u32[]{:S(2)}) collective-permute-start(bf16[2,512,512]{1,2,0:T(8,128)(2,1)} %collective-permute-done.1), channel_id=1, source_target_pairs={{2,0},{4,2},{6,4},{8,6},{10,8},{12,10},{14,12},{16,14},{18,16},{20... | collective-permute-start | bytes 3145736 | tf_op jit(solution)/shard_map/ppermute | solution.py:15
  74.1 65.2 %copy-start.8 = (bf16[1,512,512]{1,2,0:T(8,128)(2,1)}, bf16[1,512,512]{1,2,0:T(8,128)(2,1)S(1)}, u32[]{:S(2)}) copy-start(bf16[1,512,512]{1,2,0:T(8,128)(2,1)S(1)} %get-tuple-element.16) | copy-start | bytes 1572868
  74.1 22.1 %collective-permute-start.2 = (bf16[2,512,512]{1,2,0:T(8,128)(2,1)}, bf16[2,512,512]{1,2,0:T(8,128)(2,1)S(1)}, u32[]{:S(2)}, u32[]{:S(2)}) collective-permute-start(bf16[2,512,512]{1,2,0:T(8,128)(2,1)} %collective-permute-done), channel_id=1, source_target_pairs={{0,2},{2,4},{4,6},{6,8},{8,10},{10,12},{12,14},{14,16},{16,18},{18... | collective-permute-start | bytes 3145736 | tf_op jit(solution)/shard_map/ppermute | solution.py:15
  83.5 53.3 %copy-start.10 = (bf16[1,512,512]{1,2,0:T(8,128)(2,1)}, bf16[1,512,512]{1,2,0:T(8,128)(2,1)S(1)}, u32[]{:S(2)}) copy-start(bf16[1,512,512]{1,2,0:T(8,128)(2,1)S(1)} %get-tuple-element.18) | copy-start | bytes 1572868
  91.5 37.0 %copy-start.12 = (bf16[1,512,512]{1,2,0:T(8,128)(2,1)}, bf16[1,512,512]{1,2,0:T(8,128)(2,1)S(1)}, u32[]{:S(2)}) copy-start(bf16[1,512,512]{1,2,0:T(8,128)(2,1)S(1)} %get-tuple-element.20) | copy-start | bytes 1572868
  96.3 45.4 %copy-start.13 = (bf16[1,512,512]{1,2,0:T(8,128)(2,1)}, bf16[1,512,512]{1,2,0:T(8,128)(2,1)S(1)}, u32[]{:S(2)}) copy-start(bf16[1,512,512]{1,2,0:T(8,128)(2,1)S(1)} %get-tuple-element.14) | copy-start | bytes 1572868
  128.5 5.8 %copy-start.6 = (bf16[512,8,64]{0,2,1:T(8,128)(2,1)S(1)}, bf16[512,8,64]{0,2,1:T(8,128)(2,1)}, u32[]{:S(2)}) copy-start(bf16[512,8,64]{0,2,1:T(8,128)(2,1)} %reshape_squeeze.53) | copy-start | bytes 1572868
  161.3 3.3 %copy-start.9 = (bf16[1,512,512]{1,2,0:T(8,128)(2,1)S(1)}, bf16[1,512,512]{1,2,0:T(8,128)(2,1)}, u32[]{:S(2)}) copy-start(bf16[1,512,512]{1,2,0:T(8,128)(2,1)} %copy-done.8) | copy-start | bytes 1572868
  169.4 3.3 %copy-start.11 = (bf16[1,512,512]{1,2,0:T(8,128)(2,1)S(1)}, bf16[1,512,512]{1,2,0:T(8,128)(2,1)}, u32[]{:S(2)}) copy-start(bf16[1,512,512]{1,2,0:T(8,128)(2,1)} %copy-done.10) | copy-start | bytes 1572868
  182.1 3.7 %copy-start.15 = (bf16[1,512,8,64]{1,3,2,0:T(8,128)(2,1)S(1)}, bf16[1,512,8,64]{1,3,2,0:T(8,128)(2,1)}, u32[]{:S(2)}) copy-start(bf16[1,512,8,64]{1,3,2,0:T(8,128)(2,1)} %fusion.26) | copy-start | bytes 1572868
  182.1 6.7 %copy-start.2 = (bf16[8,512,512]{1,2,0:T(8,128)(2,1)S(1)}, bf16[8,512,512]{1,2,0:T(8,128)(2,1)}, u32[]{:S(2)}) copy-start(bf16[8,512,512]{1,2,0:T(8,128)(2,1)} %multiply_convert_fusion.1) | copy-start | bytes 12582916
  183.5 6.7 %copy-start.14 = (bf16[1,512,8,64]{1,3,2,0:T(8,128)(2,1)S(1)}, bf16[1,512,8,64]{1,3,2,0:T(8,128)(2,1)}, u32[]{:S(2)}) copy-start(bf16[1,512,8,64]{1,3,2,0:T(8,128)(2,1)} %fusion.24) | copy-start | bytes 1572868
  184.4 10.5 %copy-start.4 = (bf16[8,512,512]{1,2,0:T(8,128)(2,1)S(1)}, bf16[8,512,512]{1,2,0:T(8,128)(2,1)}, u32[]{:S(2)}) copy-start(bf16[8,512,512]{1,2,0:T(8,128)(2,1)} %multiply_convert_fusion.2) | copy-start | bytes 12582916
  185.8 10.5 %copy-start.17 = (bf16[1,512,8,64]{1,3,2,0:T(8,128)(2,1)S(1)}, bf16[1,512,8,64]{1,3,2,0:T(8,128)(2,1)}, u32[]{:S(2)}) copy-start(bf16[1,512,8,64]{1,3,2,0:T(8,128)(2,1)} %fusion.22) | copy-start | bytes 1572868
  186.8 30.2 %collective-permute-start.7 = (bf16[2,512,8,64]{1,3,2,0:T(8,128)(2,1)}, bf16[2,512,8,64]{1,3,2,0:T(8,128)(2,1)}, u32[]{:S(2)}, u32[]{:S(2)}) collective-permute-start(bf16[2,512,8,64]{1,3,2,0:T(8,128)(2,1)} %pad_maximum_fusion.6), channel_id=1, source_target_pairs={{0,4},{2,6},{4,8},{6,10},{8,12},{10,14},{12,16},{14,18},{16,20},{1... | collective-permute-start | bytes 3145736 | tf_op jit(solution)/shard_map/ppermute | solution.py:15
  190.2 19.6 %copy-start.16 = (bf16[1,512,8,64]{1,3,2,0:T(8,128)(2,1)S(1)}, bf16[1,512,8,64]{1,3,2,0:T(8,128)(2,1)}, u32[]{:S(2)}) copy-start(bf16[1,512,8,64]{1,3,2,0:T(8,128)(2,1)} %fusion.20) | copy-start | bytes 1572868
  191.3 26.3 %collective-permute-start.6 = (bf16[2,512,8,64]{1,3,2,0:T(8,128)(2,1)}, bf16[2,512,8,64]{1,3,2,0:T(8,128)(2,1)}, u32[]{:S(2)}, u32[]{:S(2)}) collective-permute-start(bf16[2,512,8,64]{1,3,2,0:T(8,128)(2,1)} %pad_maximum_fusion.5), channel_id=1, source_target_pairs={{4,0},{6,2},{8,4},{10,6},{12,8},{14,10},{16,12},{18,14},{20,16},{2... | collective-permute-start | bytes 3145736 | tf_op jit(solution)/shard_map/ppermute | solution.py:15
  197.3 25.9 %collective-permute-start.5 = (bf16[2,512,8,64]{1,3,2,0:T(8,128)(2,1)}, bf16[2,512,8,64]{1,3,2,0:T(8,128)(2,1)}, u32[]{:S(2)}, u32[]{:S(2)}) collective-permute-start(bf16[2,512,8,64]{1,3,2,0:T(8,128)(2,1)} %pad_maximum_fusion.4), channel_id=1, source_target_pairs={{0,2},{2,4},{4,6},{6,8},{8,10},{10,12},{12,14},{14,16},{16,18},{18... | collective-permute-start | bytes 3145736 | tf_op jit(solution)/shard_map/ppermute | solution.py:15
  210.9 22.9 %collective-permute-start.4 = (bf16[2,512,8,64]{1,3,2,0:T(8,128)(2,1)}, bf16[2,512,8,64]{1,3,2,0:T(8,128)(2,1)}, u32[]{:S(2)}, u32[]{:S(2)}) collective-permute-start(bf16[2,512,8,64]{1,3,2,0:T(8,128)(2,1)} %pad_maximum_fusion.3), channel_id=1, source_target_pairs={{2,0},{4,2},{6,4},{8,6},{10,8},{12,10},{14,12},{16,14},{18,16},{20... | collective-permute-start | bytes 3145736 | tf_op jit(solution)/shard_map/ppermute | solution.py:15
  241.1 36.2 %copy-start.1 = (s32[512,16]{0,1:T(8,128)S(1)}, s32[512,16]{0,1:T(8,128)}, u32[]{:S(2)}) copy-start(s32[512,16]{0,1:T(8,128)} %param.10) | copy-start | bytes 98308
  (3 other events, 6.1 us)
where the time goes:
time: 282 us; the launch traced here: 278 us
  matrix products  91.4 us (32%)
  waiting for transfers between devices  46.1 us (16%)
  local copies, waits for them, and re-layouts  42.5 us (15%)
  starting transfers between devices  42.5 us (15%)
  other arithmetic  28.3 us (10%)
  blocking collectives  25.3 us (9%)
    ppermute x8, starting transfers between devices, shifted(): return lax.ppermute(shard, axis, pairs)  38.5 us
    all_to_all x1, blocking collectives, on_device(): lax.all_to_all(jnp.stack([query_out, key_out, value_out]), 'head', split_...  25.3 us
    dot_general x5, matrix products, score_grads(): jnp.einsum('qhd,khd->hqk', dout_heads, value_heads, preferred_element_typ...  25.3 us
    all_to_all x1, waiting for transfers between devices, on_device(): lax.all_to_all(entering, 'head', split_axis=2, concat_axis=1, tiled=True)  24.4 us
    dot_general x5, matrix products, key_value_grads(): jnp.einsum('hqk,qhd->khd', probs.astype(jnp.bfloat16), dout_heads, prefer...  22.1 us
    ppermute x8, waiting for transfers between devices, shifted(): return lax.ppermute(shard, axis, pairs)  21.6 us
    dot_general x5, matrix products, on_device(): jnp.einsum('hqk,khd->qhd', probs.astype(jnp.bfloat16), split_heads(remote...  19.1 us
    reduce_sum x3, other arithmetic, on_device(): row_total = row_total * jnp.exp(row_top - new_top) + jnp.sum(kept, axis=-1)  14.4 us
  transfers between devices with their start and end apart: 9, of which 5 were waited for; matrix products, arithmetic and copies ran while one was open for 15% of the time, Pallas kernels for 0%

commit v1 on v0

--- a/solution.py
+++ b/solution.py
@@ -138,8 +138,16 @@
     query_out = (query_grad * score_scale).astype(jnp.bfloat16).reshape(frames, feature_cols)
     key_out = (collected[0] * score_scale).astype(jnp.bfloat16).reshape(frames, feature_cols)
     value_out = collected[1].astype(jnp.bfloat16).reshape(frames, feature_cols)
-    leaving = lax.all_to_all(
-        jnp.stack([query_out, key_out, value_out]), "head", split_axis=1, concat_axis=2, tiled=True
+    leaving = jnp.concatenate(
+        lax.all_to_all(
+            jnp.stack(
+                jnp.split(jnp.stack([query_out, key_out, value_out]), lax.axis_size("head"), axis=1)
+            ),
+            "head",
+            0,
+            0,
+        ),
+        axis=2,
     )
     return (leaving[0], leaving[1], leaving[2])
 

time: 282 us -> 262 us (0.929)
  other arithmetic: 28.3 us -> 18.2 us
  blocking collectives: 25.3 us -> 15.4 us
  local copies, waits for them, and re-layouts: 42.5 us -> 34.3 us
  waiting for transfers between devices: 46.1 us -> 52.9 us
    all_to_all x1, blocking collectives: 25.3 us -> 15.4 us  [on_device(): lax.all_to_all(jnp.stack(jnp.split(jnp.stack([query_out, key_out, value_o...]
    ppermute x8, waiting for transfers between devices: 21.6 us -> 28.4 us  [shifted(): return lax.ppermute(shard, axis, pairs)]
    slice x4 -> x1, local copies, waits for them, and re-layouts: 4.68 us -> 0.1 us  [on_device(): return (leaving[0], leaving[1], leaving[2])]
    another operation x5, other arithmetic: 4.4 us -> 0.49 us  [key_value_grads(): return jnp.stack([key_part, value_part]).astype(jnp.bfloat16)]
    another operation x1, other arithmetic: 3.57 us -> 0.17 us  [on_device(): jnp.stack([query_out, key_out, value_out])]
    convert_element_type x2 -> x0, local copies, waits for them, and re-layouts: 3.29 us -> none  [the longest x1 2.41 us: on_device(): (collected[0] * score_scale).astype(jnp.bfloat16)]
    squeeze x0 -> x3, local copies, waits for them, and re-layouts: none -> 3 us  [on_device(): return (leaving[0], leaving[1], leaving[2])]
where the time goes in v1:
time: 262 us; the launch traced here: 256 us
  matrix products  91.4 us (35%)
  waiting for transfers between devices  52.9 us (20%)
  starting transfers between devices  42.7 us (16%)
  local copies, waits for them, and re-layouts  34.3 us (13%)
  other arithmetic  18.2 us (7%)
  blocking collectives  15.4 us (6%)
    ppermute x8, starting transfers between devices, shifted(): return lax.ppermute(shard, axis, pairs)  38.7 us
    ppermute x8, waiting for transfers between devices, shifted(): return lax.ppermute(shard, axis, pairs)  28.4 us
    dot_general x5, matrix products, score_grads(): jnp.einsum('qhd,khd->hqk', dout_heads, value_heads, preferred_element_typ...  25.3 us
    all_to_all x1, waiting for transfers between devices, on_device(): lax.all_to_all(entering, 'head', split_axis=2, concat_axis=1, tiled=True)  24.4 us
    dot_general x5, matrix products, key_value_grads(): jnp.einsum('hqk,qhd->khd', probs.astype(jnp.bfloat16), dout_heads, prefer...  22.1 us
    dot_general x5, matrix products, on_device(): jnp.einsum('hqk,khd->qhd', probs.astype(jnp.bfloat16), split_heads(remote...  19.1 us
    all_to_all x1, blocking collectives, on_device(): lax.all_to_all(jnp.stack(jnp.split(jnp.stack([query_out, key_out, value_o...  15.4 us
    reduce_sum x3, other arithmetic, on_device(): row_total = row_total * jnp.exp(row_top - new_top) + jnp.sum(kept, axis=-1)  14.3 us
  transfers between devices with their start and end apart: 9, of which 5 were waited for; matrix products, arithmetic and copies ran while one was open for 15% of the time, Pallas kernels for 0%

profile of v1, /device:TPU:121, one launch (start us, length us, event | category | flops | bytes accessed | tf_op | source)
XLA Modules:
  0.0 256.4 jit_solution(13974273214401376049)
XLA Ops:
  5.1 4.0 %all-to-all-start = ((bf16[4,256,1024]{1,0,2:T(4,128)(2,1)}), bf16[4,256,1024]{1,0,2:T(4,128)(2,1)S(1)}, u32[]{:S(2)}, u32[]{:S(2)}) async-start(bf16[4,256,1024]{1,0,2:T(4,128)(2,1)} %copy.104), calls=%async_computation | async-start | bytes 4194304 | tf_op jit(solution)/shard_map/all_to_all | solution.py:60
  10.0 24.4 %all-to-all-done = bf16[4,256,1024]{1,0,2:T(4,128)(2,1)S(1)} async-done(((bf16[4,256,1024]{1,0,2:T(4,128)(2,1)}), bf16[4,256,1024]{1,0,2:T(4,128)(2,1)S(1)}, u32[]{:S(2)}, u32[]{:S(2)}) %all-to-all-start) | async-done | bytes 2097184 | tf_op jit(solution)/shard_map/all_to_all | solution.py:60
  35.8 3.7 %copy.169 = bf16[4,256,2,512]{1,2,3,0:T(2,128)(2,1)S(1)} copy(bf16[4,256,2,512]{1,0,3,2:T(4,128)(2,1)} %bitcast.158) | data formatting | bytes 4194304 | tf_op jit(solution)/shard_map/all_to_all | solution.py:60
  41.8 3.8 %collective-permute-start.1 = (bf16[2,512,512]{1,2,0:T(8,128)(2,1)}, bf16[2,512,512]{1,2,0:T(8,128)(2,1)}, u32[]{:S(2)}, u32[]{:S(2)}) collective-permute-start(bf16[2,512,512]{1,2,0:T(8,128)(2,1)} %slice.97), channel_id=1, source_target_pairs={{2,0},{4,2},{6,4},{8,6},{10,8},{12,10},{14,12},{16,14},{18,16},{20... | collective-permute-start | bytes 3145736 | tf_op jit(solution)/shard_map/ppermute | solution.py:15
  45.7 6.2 %collective-permute-start = (bf16[2,512,512]{1,2,0:T(8,128)(2,1)}, bf16[2,512,512]{1,2,0:T(8,128)(2,1)}, u32[]{:S(2)}, u32[]{:S(2)}) collective-permute-start(bf16[2,512,512]{1,2,0:T(8,128)(2,1)} %slice.97), channel_id=1, source_target_pairs={{0,2},{2,4},{4,6},{6,8},{8,10},{10,12},{12,14},{14,16},{16,18},{18... | collective-permute-start | bytes 3145736 | tf_op jit(solution)/shard_map/ppermute | solution.py:15
  74.1 8.1 %collective-permute-start.2 = (bf16[2,512,512]{1,2,0:T(8,128)(2,1)}, bf16[2,512,512]{1,2,0:T(8,128)(2,1)S(1)}, u32[]{:S(2)}, u32[]{:S(2)}) collective-permute-start(bf16[2,512,512]{1,2,0:T(8,128)(2,1)} %collective-permute-done), channel_id=1, source_target_pairs={{0,2},{2,4},{4,6},{6,8},{8,10},{10,12},{12,14},{14,16},{16,18},{18... | collective-permute-start | bytes 3145736 | tf_op jit(solution)/shard_map/ppermute | solution.py:15
  86.5 4.9 %collective-permute-done.3 = bf16[2,512,512]{1,2,0:T(8,128)(2,1)S(1)} collective-permute-done((bf16[2,512,512]{1,2,0:T(8,128)(2,1)}, bf16[2,512,512]{1,2,0:T(8,128)(2,1)S(1)}, u32[]{:S(2)}, u32[]{:S(2)}) %collective-permute-start.3) | collective-permute-done | bytes 1048608 | tf_op jit(solution)/shard_map/ppermute | solution.py:15
  91.5 4.7 %fusion.9 = (f32[8,512]{1,0:T(8,128)S(1)}, f32[8,512,512]{1,2,0:T(8,128)}) fusion(pred[512,512]{0,1:T(8,128)(4,1)S(1)} %broadcast_in_dim.159, bf16[512,8,64]{0,2,1:T(8,128)(2,1)S(1)} %reshape_squeeze.47, bf16[512,8,64]{0,2,1:T(8,128)(2,1)S(1)} %bitcast.166), kind=kOutput, calls=%fused_computation.29 | convolution fusion | flops 274722816 | bytes 9715712 | tf_op jit(solution)/shard_map/qhd,khd->hqk/dot_general | solution.py:35
  96.3 4.7 %fusion.8 = (f32[8,512]{1,0:T(8,128)S(1)}, f32[8,512,512]{1,2,0:T(8,128)}) fusion(pred[512,512]{0,1:T(8,128)(4,1)S(1)} %broadcast_in_dim.156, bf16[512,8,64]{0,2,1:T(8,128)(2,1)S(1)} %reshape_squeeze.47, bf16[512,8,64]{0,2,1:T(8,128)(2,1)S(1)} %bitcast.160), kind=kOutput, calls=%fused_computation.28 | convolution fusion | flops 274722816 | bytes 9715712 | tf_op jit(solution)/shard_map/qhd,khd->hqk/dot_general | solution.py:35
  103.5 7.9 %select_reduce_fusion = (f32[8,512]{1,0:T(8,128)S(1)}, f32[8,512]{1,0:T(8,128)S(1)}) fusion(f32[8,512,512]{1,2,0:T(8,128)} %get-tuple-element.31, f32[8,512]{1,0:T(8,128)S(1)} %get-tuple-element.3, pred[512,512]{0,1:T(8,128)(4,1)S(1)} %broadcast_in_dim.159, f32[8,512]{1,0:T(8,128)S(1)} %get-tuple-element.4, f32[8,512,512]{1,2,0:T(8,128)} %get-tuple-element.33, ...), kind=kLoop, calls=%fused_computation.10 | loop fusion | flops 20963328 | bytes 17367040 | tf_op jit(solution)/shard_map/reduce_sum | solution.py:106
  111.4 4.0 %select_reduce_fusion.2 = (f32[8,512]{1,0:T(8,128)S(1)}, f32[8,512]{1,0:T(8,128)S(1)}) fusion(f32[8,512,512]{1,2,0:T(8,128)S(1)} %get-tuple-element.35, f32[8,512]{1,0:T(8,128)S(1)} %get-tuple-element.5, pred[512,512]{0,1:T(8,128)(4,1)S(1)} %broadcast_in_dim.153, f32[8,512]{1,0:T(8,128)S(1)} %get-tuple-element.6, f32[8,512,512]{1,2,0:T(8,128)S(1)} %get-tuple-element.37, ...), kind=kLoop, calls=%fused_computation.12 | loop fusion | flops 20963328 | bytes 17367040 | tf_op jit(solution)/shard_map/reduce_sum | solution.py:106
  115.4 6.5 %fusion.26 = bf16[1,512,8,64]{1,3,2,0:T(8,128)(2,1)} fusion(bf16[512,8,64]{0,2,1:T(8,128)(2,1)S(1)} %reshape_squeeze.52, f32[8,512,512]{1,2,0:T(8,128)} %get-tuple-element.31, f32[8,512]{1,0:T(8,128)S(1)} %log_add_fusion, pred[512,512]{0,1:T(8,128)(4,1)S(1)} %broadcast_in_dim.159), kind=kOutput, calls=%fused_computation.67 | convolution fusion | flops 279183360 | bytes 9715712 | tf_op jit(solution)/shard_map/hqk,qhd->khd/dot_general | solution.py:48
  121.9 6.5 %fusion.24 = bf16[1,512,8,64]{1,3,2,0:T(8,128)(2,1)} fusion(bf16[512,8,64]{0,2,1:T(8,128)(2,1)S(1)} %reshape_squeeze.52, f32[8,512,512]{1,2,0:T(8,128)} %get-tuple-element.33, f32[8,512]{1,0:T(8,128)S(1)} %log_add_fusion, pred[512,512]{0,1:T(8,128)(4,1)S(1)} %broadcast_in_dim.156), kind=kOutput, calls=%fused_computation.65 | convolution fusion | flops 279183360 | bytes 9715712 | tf_op jit(solution)/shard_map/hqk,qhd->khd/dot_general | solution.py:48
  128.4 5.8 %fusion.36 = f32[8,64,512]{2,1,0:T(8,128)S(1)} fusion(bf16[512,8,64]{0,2,1:T(8,128)(2,1)S(1)} %bitcast.178, f32[8,512,512]{1,2,0:T(8,128)} %get-tuple-element.31, f32[8,512]{1,0:T(8,128)S(1)} %log_add_fusion, pred[512,512]{0,1:T(8,128)(4,1)S(1)} %broadcast_in_dim.159), kind=kOutput, calls=%fused_computation.85 | convolution fusion | flops 278921216 | bytes 10240000 | tf_op jit(solution)/shard_map/hqk,khd->qhd/dot_general | solution.py:116
  141.7 5.9 %fusion.16 = f32[512,8]{0,1:T(8,128)S(1)} fusion(f32[8,64,512]{2,1,0:T(8,128)S(1)} %fusion.36, f32[8,64,512]{2,1,0:T(8,128)S(1)} %convolution_add_fusion.4, bf16[512,8,64]{0,2,1:T(8,128)(2,1)S(1)} %bitcast.180, bf16[512,8,64]{0,2,1:T(8,128)(2,1)S(1)} %reshape_squeeze.52, f32[8,512,512]{1,2,0:T(8,128)} %get-tuple-element.33, f32[8,512]{1,0:T(8,128)S(1)} %log_add_fusion, ...), kind=kOutput, calls=%fused_computation.57 | convolution fusion | flops 280227840 | bytes 11829248 | tf_op jit(solution)/shard_map/hqk,khd->qhd/dot_general | solution.py:116
  147.6 6.9 %multiply_convert_fusion = bf16[8,512,512]{1,2,0:T(8,128)(2,1)} fusion(f32[8,512,512]{1,2,0:T(8,128)} %get-tuple-element.31, f32[8,512]{1,0:T(8,128)S(1)} %bitcast.186, f32[8,512]{1,0:T(8,128)S(1)} %log_add_fusion, pred[512,512]{0,1:T(8,128)(4,1)S(1)} %broadcast_in_dim.159, bf16[512,8,64]{0,2,1:T(8,128)(2,1)S(1)} %reshape_squeeze.52, ...), kind=kOutput, calls=%fused_computation | convolution fusion | flops 283115520 | bytes 13926400 | tf_op jit(solution)/shard_map/qhd,khd->hqk/dot_general | solution.py:40
  154.4 6.8 %multiply_convert_fusion.1 = bf16[8,512,512]{1,2,0:T(8,128)(2,1)} fusion(f32[8,512,512]{1,2,0:T(8,128)} %get-tuple-element.33, f32[8,512]{1,0:T(8,128)S(1)} %bitcast.187, f32[8,512]{1,0:T(8,128)S(1)} %log_add_fusion, pred[512,512]{0,1:T(8,128)(4,1)S(1)} %broadcast_in_dim.156, bf16[512,8,64]{0,2,1:T(8,128)(2,1)S(1)} %reshape_squeeze.52, ...), kind=kOutput, calls=%fused_computation.1 | convolution fusion | flops 283115520 | bytes 13926400 | tf_op jit(solution)/shard_map/qhd,khd->hqk/dot_general | solution.py:40
  164.6 4.8 %multiply_convert_fusion.2 = bf16[8,512,512]{1,2,0:T(8,128)(2,1)} fusion(f32[8,512,512]{1,2,0:T(8,128)S(1)} %get-tuple-element.35, f32[8,512]{1,0:T(8,128)S(1)} %bitcast.188, f32[8,512]{1,0:T(8,128)S(1)} %log_add_fusion, pred[512,512]{0,1:T(8,128)(4,1)S(1)} %broadcast_in_dim.153, bf16[512,8,64]{0,2,1:T(8,128)(2,1)S(1)} %reshape_squeeze.52, ...), kind=kOutput, calls=%fused_computation.2 | convolution fusion | flops 283115520 | bytes 13926400 | tf_op jit(solution)/shard_map/qhd,khd->hqk/dot_general | solution.py:40
  178.6 3.4 %multiply_convert_fusion.4 = bf16[8,512,512]{1,2,0:T(8,128)(2,1)S(1)} fusion(f32[8,512,512]{1,2,0:T(8,128)S(1)} %get-tuple-element.39, f32[8,512]{1,0:T(8,128)S(1)} %bitcast.190, f32[8,512]{1,0:T(8,128)S(1)} %log_add_fusion, pred[512,512]{0,1:T(8,128)(4,1)S(1)} %broadcast_in_dim.145, bf16[512,8,64]{0,2,1:T(8,128)(2,1)S(1)} %reshape_squeeze.52, ...), kind=kOutput, calls=%fused_computation.4 | convolution fusion | flops 283115520 | bytes 13926400 | tf_op jit(solution)/shard_map/qhd,khd->hqk/dot_general | solution.py:40
  189.4 3.7 %collective-permute-start.6 = (bf16[2,512,8,64]{1,3,2,0:T(8,128)(2,1)S(1)}, bf16[2,512,8,64]{1,3,2,0:T(8,128)(2,1)S(1)}, u32[]{:S(2)}, u32[]{:S(2)}) collective-permute-start(bf16[2,512,8,64]{1,3,2,0:T(8,128)(2,1)S(1)} %pad_maximum_fusion.6), channel_id=1, source_target_pairs={{4,0},{6,2},{8,4},{10,6},{12,8},{14,10},{16,12},{18,14},{20,16},{2... | collective-permute-start | bytes 3145736 | tf_op jit(solution)/shard_map/ppermute | solution.py:15
  194.7 11.1 %collective-permute-start.5 = (bf16[2,512,8,64]{1,3,2,0:T(8,128)(2,1)S(1)}, bf16[2,512,8,64]{1,3,2,0:T(8,128)(2,1)S(1)}, u32[]{:S(2)}, u32[]{:S(2)}) collective-permute-start(bf16[2,512,8,64]{1,3,2,0:T(8,128)(2,1)S(1)} %pad_maximum_fusion.5), channel_id=1, source_target_pairs={{0,2},{2,4},{4,6},{6,8},{8,10},{10,12},{12,14},{14,16},{16,18},{18... | collective-permute-start | bytes 3145736 | tf_op jit(solution)/shard_map/ppermute | solution.py:15
  215.6 6.5 %collective-permute-done.5 = bf16[2,512,8,64]{1,3,2,0:T(8,128)(2,1)S(1)} collective-permute-done((bf16[2,512,8,64]{1,3,2,0:T(8,128)(2,1)S(1)}, bf16[2,512,8,64]{1,3,2,0:T(8,128)(2,1)S(1)}, u32[]{:S(2)}, u32[]{:S(2)}) %collective-permute-start.5) | collective-permute-done | bytes 1048608 | tf_op jit(solution)/shard_map/ppermute | solution.py:15
  222.1 13.9 %collective-permute-done.4 = bf16[2,512,8,64]{1,3,2,0:T(8,128)(2,1)S(1)} collective-permute-done((bf16[2,512,8,64]{1,3,2,0:T(8,128)(2,1)S(1)}, bf16[2,512,8,64]{1,3,2,0:T(8,128)(2,1)S(1)}, u32[]{:S(2)}, u32[]{:S(2)}) %collective-permute-start.4) | collective-permute-done | bytes 1048608 | tf_op jit(solution)/shard_map/ppermute | solution.py:15
  237.6 15.4 %all_to_all.20 = bf16[2,3,256,512]{2,3,1,0:T(8,128)(2,1)S(1)} all-to-all(bf16[2,3,256,512]{2,3,1,0:T(8,128)(2,1)S(1)} %pad_maximum_fusion.2), channel_id=1, replica_groups=mesh['ctx'=64,'head'=2] {'head'}, dimensions={0} | all-to-all | bytes 3145728 | tf_op jit(solution)/shard_map/all_to_all | solution.py:142
  (117 shorter events, 81.1 us)
Async XLA Ops:
  0.6 8.4 %copy-start = (s32[512,16]{0,1:T(8,128)S(1)}, s32[512,16]{0,1:T(8,128)}, u32[]{:S(2)}) copy-start(s32[512,16]{0,1:T(8,128)} %param.10) | copy-start | bytes 98308
  5.1 29.4 %all-to-all-start = ((bf16[4,256,1024]{1,0,2:T(4,128)(2,1)}), bf16[4,256,1024]{1,0,2:T(4,128)(2,1)S(1)}, u32[]{:S(2)}, u32[]{:S(2)}) async-start(bf16[4,256,1024]{1,0,2:T(4,128)(2,1)} %copy.104), calls=%async_computation | async-start | bytes 4194304 | tf_op jit(solution)/shard_map/all_to_all | solution.py:60
  41.8 29.1 %collective-permute-start.1 = (bf16[2,512,512]{1,2,0:T(8,128)(2,1)}, bf16[2,512,512]{1,2,0:T(8,128)(2,1)}, u32[]{:S(2)}, u32[]{:S(2)}) collective-permute-start(bf16[2,512,512]{1,2,0:T(8,128)(2,1)} %slice.97), channel_id=1, source_target_pairs={{2,0},{4,2},{6,4},{8,6},{10,8},{12,10},{14,12},{16,14},{18,16},{20... | collective-permute-start | bytes 3145736 | tf_op jit(solution)/shard_map/ppermute | solution.py:15
  45.7 28.4 %collective-permute-start = (bf16[2,512,512]{1,2,0:T(8,128)(2,1)}, bf16[2,512,512]{1,2,0:T(8,128)(2,1)}, u32[]{:S(2)}, u32[]{:S(2)}) collective-permute-start(bf16[2,512,512]{1,2,0:T(8,128)(2,1)} %slice.97), channel_id=1, source_target_pairs={{0,2},{2,4},{4,6},{6,8},{8,10},{10,12},{12,14},{14,16},{16,18},{18... | collective-permute-start | bytes 3145736 | tf_op jit(solution)/shard_map/ppermute | solution.py:15
  70.9 20.5 %collective-permute-start.3 = (bf16[2,512,512]{1,2,0:T(8,128)(2,1)}, bf16[2,512,512]{1,2,0:T(8,128)(2,1)S(1)}, u32[]{:S(2)}, u32[]{:S(2)}) collective-permute-start(bf16[2,512,512]{1,2,0:T(8,128)(2,1)} %collective-permute-done.1), channel_id=1, source_target_pairs={{2,0},{4,2},{6,4},{8,6},{10,8},{12,10},{14,12},{16,14},{18,16},{20... | collective-permute-start | bytes 3145736 | tf_op jit(solution)/shard_map/ppermute | solution.py:15
  74.1 65.2 %copy-start.8 = (bf16[1,512,512]{1,2,0:T(8,128)(2,1)}, bf16[1,512,512]{1,2,0:T(8,128)(2,1)S(1)}, u32[]{:S(2)}) copy-start(bf16[1,512,512]{1,2,0:T(8,128)(2,1)S(1)} %get-tuple-element.18) | copy-start | bytes 1572868
  74.1 22.1 %collective-permute-start.2 = (bf16[2,512,512]{1,2,0:T(8,128)(2,1)}, bf16[2,512,512]{1,2,0:T(8,128)(2,1)S(1)}, u32[]{:S(2)}, u32[]{:S(2)}) collective-permute-start(bf16[2,512,512]{1,2,0:T(8,128)(2,1)} %collective-permute-done), channel_id=1, source_target_pairs={{0,2},{2,4},{4,6},{6,8},{8,10},{10,12},{12,14},{14,16},{16,18},{18... | collective-permute-start | bytes 3145736 | tf_op jit(solution)/shard_map/ppermute | solution.py:15
  83.4 53.3 %copy-start.10 = (bf16[1,512,512]{1,2,0:T(8,128)(2,1)}, bf16[1,512,512]{1,2,0:T(8,128)(2,1)S(1)}, u32[]{:S(2)}) copy-start(bf16[1,512,512]{1,2,0:T(8,128)(2,1)S(1)} %get-tuple-element.20) | copy-start | bytes 1572868
  91.5 36.9 %copy-start.12 = (bf16[1,512,512]{1,2,0:T(8,128)(2,1)}, bf16[1,512,512]{1,2,0:T(8,128)(2,1)S(1)}, u32[]{:S(2)}) copy-start(bf16[1,512,512]{1,2,0:T(8,128)(2,1)S(1)} %get-tuple-element.22) | copy-start | bytes 1572868
  96.3 45.4 %copy-start.13 = (bf16[1,512,512]{1,2,0:T(8,128)(2,1)}, bf16[1,512,512]{1,2,0:T(8,128)(2,1)S(1)}, u32[]{:S(2)}) copy-start(bf16[1,512,512]{1,2,0:T(8,128)(2,1)S(1)} %get-tuple-element.16) | copy-start | bytes 1572868
  128.4 5.8 %copy-start.6 = (bf16[512,8,64]{0,2,1:T(8,128)(2,1)S(1)}, bf16[512,8,64]{0,2,1:T(8,128)(2,1)}, u32[]{:S(2)}) copy-start(bf16[512,8,64]{0,2,1:T(8,128)(2,1)} %reshape_squeeze.53) | copy-start | bytes 1572868
  161.3 3.3 %copy-start.9 = (bf16[1,512,512]{1,2,0:T(8,128)(2,1)S(1)}, bf16[1,512,512]{1,2,0:T(8,128)(2,1)}, u32[]{:S(2)}) copy-start(bf16[1,512,512]{1,2,0:T(8,128)(2,1)} %copy-done.8) | copy-start | bytes 1572868
  169.3 3.3 %copy-start.11 = (bf16[1,512,512]{1,2,0:T(8,128)(2,1)S(1)}, bf16[1,512,512]{1,2,0:T(8,128)(2,1)}, u32[]{:S(2)}) copy-start(bf16[1,512,512]{1,2,0:T(8,128)(2,1)} %copy-done.10) | copy-start | bytes 1572868
  182.0 3.7 %copy-start.15 = (bf16[1,512,8,64]{1,3,2,0:T(8,128)(2,1)S(1)}, bf16[1,512,8,64]{1,3,2,0:T(8,128)(2,1)}, u32[]{:S(2)}) copy-start(bf16[1,512,8,64]{1,3,2,0:T(8,128)(2,1)} %fusion.26) | copy-start | bytes 1572868
  182.0 5.8 %copy-start.2 = (bf16[8,512,512]{1,2,0:T(8,128)(2,1)S(1)}, bf16[8,512,512]{1,2,0:T(8,128)(2,1)}, u32[]{:S(2)}) copy-start(bf16[8,512,512]{1,2,0:T(8,128)(2,1)} %multiply_convert_fusion.1) | copy-start | bytes 12582916
  183.4 5.8 %copy-start.14 = (bf16[1,512,8,64]{1,3,2,0:T(8,128)(2,1)S(1)}, bf16[1,512,8,64]{1,3,2,0:T(8,128)(2,1)}, u32[]{:S(2)}) copy-start(bf16[1,512,8,64]{1,3,2,0:T(8,128)(2,1)} %fusion.24) | copy-start | bytes 1572868
  184.3 8.9 %copy-start.4 = (bf16[8,512,512]{1,2,0:T(8,128)(2,1)S(1)}, bf16[8,512,512]{1,2,0:T(8,128)(2,1)}, u32[]{:S(2)}) copy-start(bf16[8,512,512]{1,2,0:T(8,128)(2,1)} %multiply_convert_fusion.2) | copy-start | bytes 12582916
  185.7 8.8 %copy-start.17 = (bf16[1,512,8,64]{1,3,2,0:T(8,128)(2,1)S(1)}, bf16[1,512,8,64]{1,3,2,0:T(8,128)(2,1)}, u32[]{:S(2)}) copy-start(bf16[1,512,8,64]{1,3,2,0:T(8,128)(2,1)} %fusion.22) | copy-start | bytes 1572868
  185.8 26.7 %collective-permute-start.7 = (bf16[2,512,8,64]{1,3,2,0:T(8,128)(2,1)S(1)}, bf16[2,512,8,64]{1,3,2,0:T(8,128)(2,1)S(1)}, u32[]{:S(2)}, u32[]{:S(2)}) collective-permute-start(bf16[2,512,8,64]{1,3,2,0:T(8,128)(2,1)S(1)} %pad_maximum_fusion.7), channel_id=1, source_target_pairs={{0,4},{2,6},{4,8},{6,10},{8,12},{10,14},{12,16},{14,18},{16,20},{1... | collective-permute-start | bytes 3145736 | tf_op jit(solution)/shard_map/ppermute | solution.py:15
  189.3 17.8 %copy-start.16 = (bf16[1,512,8,64]{1,3,2,0:T(8,128)(2,1)S(1)}, bf16[1,512,8,64]{1,3,2,0:T(8,128)(2,1)}, u32[]{:S(2)}) copy-start(bf16[1,512,8,64]{1,3,2,0:T(8,128)(2,1)} %fusion.20) | copy-start | bytes 1572868
  189.4 26.1 %collective-permute-start.6 = (bf16[2,512,8,64]{1,3,2,0:T(8,128)(2,1)S(1)}, bf16[2,512,8,64]{1,3,2,0:T(8,128)(2,1)S(1)}, u32[]{:S(2)}, u32[]{:S(2)}) collective-permute-start(bf16[2,512,8,64]{1,3,2,0:T(8,128)(2,1)S(1)} %pad_maximum_fusion.6), channel_id=1, source_target_pairs={{4,0},{6,2},{8,4},{10,6},{12,8},{14,10},{16,12},{18,14},{20,16},{2... | collective-permute-start | bytes 3145736 | tf_op jit(solution)/shard_map/ppermute | solution.py:15
  194.7 27.4 %collective-permute-start.5 = (bf16[2,512,8,64]{1,3,2,0:T(8,128)(2,1)S(1)}, bf16[2,512,8,64]{1,3,2,0:T(8,128)(2,1)S(1)}, u32[]{:S(2)}, u32[]{:S(2)}) collective-permute-start(bf16[2,512,8,64]{1,3,2,0:T(8,128)(2,1)S(1)} %pad_maximum_fusion.5), channel_id=1, source_target_pairs={{0,2},{2,4},{4,6},{6,8},{8,10},{10,12},{12,14},{14,16},{16,18},{18... | collective-permute-start | bytes 3145736 | tf_op jit(solution)/shard_map/ppermute | solution.py:15
  207.2 28.8 %collective-permute-start.4 = (bf16[2,512,8,64]{1,3,2,0:T(8,128)(2,1)S(1)}, bf16[2,512,8,64]{1,3,2,0:T(8,128)(2,1)S(1)}, u32[]{:S(2)}, u32[]{:S(2)}) collective-permute-start(bf16[2,512,8,64]{1,3,2,0:T(8,128)(2,1)S(1)} %pad_maximum_fusion.4), channel_id=1, source_target_pairs={{2,0},{4,2},{6,4},{8,6},{10,8},{12,10},{14,12},{16,14},{18,16},{20... | collective-permute-start | bytes 3145736 | tf_op jit(solution)/shard_map/ppermute | solution.py:15
  237.1 19.0 %copy-start.1 = (s32[512,16]{0,1:T(8,128)S(1)}, s32[512,16]{0,1:T(8,128)}, u32[]{:S(2)}) copy-start(s32[512,16]{0,1:T(8,128)} %param.10) | copy-start | bytes 98308
  (3 other events, 6.1 us)
